TPU v7x, 128 devices: a whole 4x4x4 slice. The times are simulated.
128 devices in a mesh: segment: 2 (over z_hi), win: 16 (over y, z_lo, core), head: 4 (over x).
Axes of the slice: x: 4, y: 4, z: 4 (z_hi: 2, z_lo: 2; z = z_hi * 2 + z_lo), core: 2. Of those that a mesh axis runs over, the one named last changes fastest.
Arguments:
- inputs: bfloat16 [2, 30, 480, 1536], P(None, None, 'win', 'head'), may hold values from -16 to 16
- gains: float32 [2, 1536], P('segment'), may hold values from 0.1 to 1.9
- qkv_weight: bfloat16 [2, 1536, 3, 1536], P('segment', None, None, 'head'), may hold values from -3.5 to 3.5
- out_weight: bfloat16 [2, 1536, 1536], P('segment', 'head'), may hold values from -0.15625 to 0.15625
- labels: int32 [30, 480], P(None, 'win'), may hold values from 0 to 3, as said below
Outputs:
- sections: bfloat16 [2, 2, 30, 480, 1536], P('segment', None, None, 'win', 'head')
Inputs may be any that keep to these rules, and one draw needn't show every extreme that they name: In each window of 30 by 30 cells the label is 2 on the rows from a drawn row cut on plus 1 on the columns from a drawn column cut on; both cuts lie in 1 to 29, so every window holds all four labels.
All inputs are finite; a program needn't handle non-finite values.
Results may differ from a plain program's by a relative error of at most 0.013.
Values may be sent and summed in bfloat16 or wider, within the bound.
No kernel may reach another device: no remote copies, remote signals or barrier semaphores. Data moves between devices by JAX's collectives and lax.ppermute only.
A program may use at most 128 MiB of HBM per device.

v0:
```python
import jax
import jax.numpy as jnp
from jax import lax
from jax.sharding import PartitionSpec as P

HEAD_DIM = 128
WIN_SIDE = 30


def passed_along(array, axis, by):
    length = lax.axis_size(axis)
    return lax.ppermute(array, axis, [(i, (i + by) % length) for i in range(length)])


def shifted(value, axis, steps):
    count = lax.axis_size(axis)
    first, last = (max(0, -steps), min(count, count - steps))
    return lax.ppermute(value, axis, [(source, source + steps) for source in range(first, last)])


def rms_normed(slab, gain_row):
    values_f = slab.astype(jnp.float32)
    mean_square = jnp.mean(values_f * values_f, axis=-1, keepdims=True)
    return (values_f * lax.rsqrt(mean_square + 1e-05) * gain_row).astype(jnp.bfloat16)


def to_windows(grid):
    win_rows = grid.shape[0]
    win_count = grid.shape[1] // win_rows
    features = grid.shape[2]
    return (
        grid.reshape(win_rows, win_count, win_rows, features)
        .transpose(1, 0, 2, 3)
        .reshape(win_count, win_rows * win_rows, features)
    )


def from_windows(blocks, win_rows):
    win_count = blocks.shape[0]
    features = blocks.shape[2]
    return (
        blocks.reshape(win_count, win_rows, win_rows, features)
        .transpose(1, 0, 2, 3)
        .reshape(win_rows, win_count * win_rows, features)
    )


def window_layer(current, gain_row, qkv_local, allowed, project):
    gathered = lax.all_gather(current, "head", axis=2, tiled=True)
    normed = rms_normed(gathered, gain_row)
    win_normed = to_windows(normed)
    projected_qkv = jnp.einsum(
        "wtd,dcf->wtcf", win_normed, qkv_local, preferred_element_type=jnp.float32
    ).astype(jnp.bfloat16)
    win_count = projected_qkv.shape[0]
    tokens = projected_qkv.shape[1]
    local_feat = projected_qkv.shape[3]
    heads_local = local_feat // HEAD_DIM
    split_qkv = projected_qkv.reshape(win_count, tokens, 3, heads_local, HEAD_DIM)
    queries = split_qkv[:, :, 0]
    keys_all = split_qkv[:, :, 1]
    values_all = split_qkv[:, :, 2]
    scores = jnp.einsum(
        "wqhe,wkhe->whqk", queries, keys_all, preferred_element_type=jnp.float32
    ) * HEAD_DIM ** (-0.5)
    scores = jnp.where(allowed[:, None], scores, -1e30)
    top_score = jnp.max(scores, axis=-1, keepdims=True)
    expo = jnp.exp(scores - top_score)
    attn_prob = (expo / jnp.sum(expo, axis=-1, keepdims=True)).astype(jnp.bfloat16)
    attended = jnp.einsum(
        "whqk,wkhe->wqhe", attn_prob, values_all, preferred_element_type=jnp.float32
    ).astype(jnp.bfloat16)
    attended = attended.reshape(win_count, tokens, local_feat)
    grid_att = from_windows(attended, current.shape[0])
    projected = project(grid_att)
    return (current.astype(jnp.float32) + projected).astype(jnp.bfloat16)


def body(inputs, gains, qkv_weight, out_weight, labels):
    segment_id = lax.axis_index("segment")
    micro_count = inputs.shape[0]
    gain_row = gains[0]
    qkv_local = qkv_weight[0]
    out_local = out_weight[0]
    win_labels = to_windows(labels[:, :, None])[:, :, 0]
    allowed = (win_labels[:, :, None] == win_labels[:, None, :]) | (segment_id == 0)
    half_cols = WIN_SIDE // 2

    def project(grid_att):
        partial_sum = jnp.einsum(
            "rcf,fg->rcg", grid_att, out_local, preferred_element_type=jnp.float32
        )
        return lax.psum_scatter(
            partial_sum.astype(jnp.bfloat16), "head", scatter_dimension=2, tiled=True
        ).astype(jnp.float32)

    def advance(incoming, step_id):
        fresh = lax.dynamic_index_in_dim(
            inputs, jnp.minimum(step_id, micro_count - 1), 0, keepdims=False
        )
        current = jnp.where(segment_id == 0, fresh, incoming)
        leading = passed_along(current[:, :half_cols], "win", -1)
        rolled = jnp.concatenate([current[:, half_cols:], leading], axis=1)
        current = jnp.where(segment_id == 1, rolled, current)
        result = window_layer(current, gain_row, qkv_local, allowed, project)
        passed = shifted(result, "segment", 1)
        return (passed, result)

    start_slab = jnp.zeros(inputs.shape[1:], jnp.bfloat16)
    _, produced = lax.scan(advance, start_slab, jnp.arange(micro_count + 1, dtype=jnp.int32))
    sections = lax.dynamic_slice_in_dim(produced, segment_id, micro_count, 0)
    return sections[None]


def solution(mesh):
    in_specs = (
        P(None, None, "win", "head"),
        P("segment", None),
        P("segment", None, None, "head"),
        P("segment", "head", None),
        P(None, "win"),
    )
    out_specs = P("segment", None, None, "win", "head")
    return jax.shard_map(body, mesh=mesh, in_specs=in_specs, out_specs=out_specs, check_vma=False)
```

profile of v0, /device:TPU:0, one launch (start us, length us, event | category | flops | bytes accessed | tf_op | source)
XLA Modules:
  0.0 619.6 jit_solution(4641840400463781002)
XLA Ops:
  10.2 598.5 %while.16 = (s32[]{:T(128)}, bf16[30,30,384]{2,1,0:T(8,128)(2,1)S(1)}, bf16[3,30,30,384]{3,2,1,0:T(8,128)(2,1)}, pred[]{:T(512)}, pred[]{:T(512)}, /*index=5*/s3...) while((s32[]{:T(128)}, ...), condition=%wide.region_5.6_spmd.clone.clone, body=%wide.region_0.5_spmd.clone.clone.sunk | while | flops 5522992128 | bytes 120185344 | solution.py:110
  16.8 5.0 collective-permute-done
  24.8 38.2 %all-gather.2.cloned.1.call-done = bf16[30,30,1536]{2,1,0:T(8,128)(2,1)} async-done(((bf16[30,30,384]{2,1,0:T(8,128)(2,1)}), bf16[30,30,1536]{2,1,0:T(8,128)(2,1)}) %all-gather.2.cloned.1.call-update) | async-done | bytes 2764816 | tf_op jit(solution)/shard_map/while/body/eval_jaxpr/all_gather | solution.py:49
  68.7 7.9 %convolution_convert_fusion.4 = bf16[900,3,384]{2,0,1:T(8,128)(2,1)} fusion(bf16[900,1536,1]{1,0,2:T(8,128)(2,1)} %reshape.166, bf16[1536,3,384]{2,0,1:T(8,128)(2,1)} %get-tuple-element.361), kind=kOutput, calls=%fused_computation.17.clone.1 | convolution fusion | flops 3186086400 | bytes 8377344 | tf_op jit(solution)/shard_map/while/body/eval_jaxpr/wtd,dcf->wtcf/dot_general | solution.py:52
  79.5 7.3 %fusion.40 = (f32[3,900]{1,0:T(4,128)S(1)}, f32[3,900,900]{1,2,0:T(8,128)}) fusion(pred[900,900]{0,1:T(8,128)(4,1)S(1)} %copy-done.1, bf16[1,900,3,3,128]{1,4,3,2,0:T(8,128)(2,1)S(1)} %bitcast.85), kind=kOutput, calls=%fused_computation.36.clone.1 | convolution fusion | flops 631800960 | bytes 12229360 | tf_op jit(solution)/shard_map/while/body/eval_jaxpr/sub | solution.py:68
  86.8 6.4 %fusion.41 = bf16[1,900,3,128]{3,1,2,0:T(8,128)(2,1)S(1)} fusion(f32[3,900,900]{1,2,0:T(8,128)} %get-tuple-element.317, f32[3,900]{1,0:T(4,128)S(1)} %get-tuple-element.318, bf16[1,900,3,3,128]{1,4,3,2,0:T(8,128)(2,1)S(1)} %bitcast.86), kind=kOutput, calls=%fused_computation.20.clone.1 | convolution fusion | flops 627285632 | bytes 11214016 | tf_op jit(solution)/shard_map/while/body/eval_jaxpr/whqk,wkhe->wqhe/dot_general | solution.py:70
  98.1 18.7 %copy.42 = bf16[30,30,1536]{1,0,2:T(8,128)(2,1)} copy(bf16[30,30,1536]{2,1,0:T(8,128)(2,1)S(1)} %convolution_convert_fusion.5) | data formatting | bytes 5529600 | tf_op jit(solution)/shard_map/while
  116.8 20.3 %reshape.168 = bf16[1536,900]{1,0:T(8,128)(2,1)} reshape(bf16[1536,30,30]{2,1,0:T(8,128)(2,1)} %bitcast.83) | data formatting | bytes 5529600 | tf_op jit(solution)/shard_map/while
  137.1 38.6 %reduce-scatter.6.cloned.1.call-done = bf16[384,900]{1,0:T(8,128)(2,1)} async-done(((bf16[1536,900]{1,0:T(8,128)(2,1)}), bf16[384,900]{1,0:T(8,128)(2,1)}) %reduce-scatter.6.cloned.1.call-update) | async-done | bytes 691216 | tf_op jit(solution)/shard_map/while
  175.7 8.9 %reshape.169 = bf16[384,30,30]{2,1,0:T(8,128)(2,1)S(1)} reshape(bf16[384,900]{1,0:T(8,128)(2,1)} %reduce-scatter.6.cloned.1.call-done) | data formatting | bytes 1382400 | tf_op jit(solution)/shard_map/while
  191.1 5.1 collective-permute-start.1
  196.2 15.6 %collective-permute-done.1 = bf16[30,30,384]{2,1,0:T(8,128)(2,1)S(1)} collective-permute-done((bf16[30,30,384]{2,1,0:T(8,128)(2,1)S(1)}, bf16[30,30,384]{2,1,0:T(8,128)(2,1)S(1)}, u32[]{:S(2)}, u32[]{:S(2)}) %collective-permute-start.1) | collective-permute-done | bytes 691232 | tf_op jit(solution)/shard_map/while/body/eval_jaxpr/ppermute | solution.py:18
  223.8 37.6 %all-gather.2.cloned.1.call-done = bf16[30,30,1536]{2,1,0:T(8,128)(2,1)} async-done(((bf16[30,30,384]{2,1,0:T(8,128)(2,1)}), bf16[30,30,1536]{2,1,0:T(8,128)(2,1)}) %all-gather.2.cloned.1.call-update) | async-done | bytes 2764816 | tf_op jit(solution)/shard_map/while/body/eval_jaxpr/all_gather | solution.py:49
  267.2 7.9 %convolution_convert_fusion.4 = bf16[900,3,384]{2,0,1:T(8,128)(2,1)} fusion(bf16[900,1536,1]{1,0,2:T(8,128)(2,1)} %reshape.166, bf16[1536,3,384]{2,0,1:T(8,128)(2,1)} %get-tuple-element.361), kind=kOutput, calls=%fused_computation.17.clone.1 | convolution fusion | flops 3186086400 | bytes 8377344 | tf_op jit(solution)/shard_map/while/body/eval_jaxpr/wtd,dcf->wtcf/dot_general | solution.py:52
  278.0 7.4 %fusion.40 = (f32[3,900]{1,0:T(4,128)S(1)}, f32[3,900,900]{1,2,0:T(8,128)}) fusion(pred[900,900]{0,1:T(8,128)(4,1)S(1)} %copy-done.1, bf16[1,900,3,3,128]{1,4,3,2,0:T(8,128)(2,1)S(1)} %bitcast.85), kind=kOutput, calls=%fused_computation.36.clone.1 | convolution fusion | flops 631800960 | bytes 12229360 | tf_op jit(solution)/shard_map/while/body/eval_jaxpr/sub | solution.py:68
  285.3 6.4 %fusion.41 = bf16[1,900,3,128]{3,1,2,0:T(8,128)(2,1)S(1)} fusion(f32[3,900,900]{1,2,0:T(8,128)} %get-tuple-element.317, f32[3,900]{1,0:T(4,128)S(1)} %get-tuple-element.318, bf16[1,900,3,3,128]{1,4,3,2,0:T(8,128)(2,1)S(1)} %bitcast.86), kind=kOutput, calls=%fused_computation.20.clone.1 | convolution fusion | flops 627285632 | bytes 11214016 | tf_op jit(solution)/shard_map/while/body/eval_jaxpr/whqk,wkhe->wqhe/dot_general | solution.py:70
  296.6 18.7 %copy.42 = bf16[30,30,1536]{1,0,2:T(8,128)(2,1)} copy(bf16[30,30,1536]{2,1,0:T(8,128)(2,1)S(1)} %convolution_convert_fusion.5) | data formatting | bytes 5529600 | tf_op jit(solution)/shard_map/while
  315.3 20.3 %reshape.168 = bf16[1536,900]{1,0:T(8,128)(2,1)} reshape(bf16[1536,30,30]{2,1,0:T(8,128)(2,1)} %bitcast.83) | data formatting | bytes 5529600 | tf_op jit(solution)/shard_map/while
  335.6 38.6 %reduce-scatter.6.cloned.1.call-done = bf16[384,900]{1,0:T(8,128)(2,1)} async-done(((bf16[1536,900]{1,0:T(8,128)(2,1)}), bf16[384,900]{1,0:T(8,128)(2,1)}) %reduce-scatter.6.cloned.1.call-update) | async-done | bytes 691216 | tf_op jit(solution)/shard_map/while
  374.2 8.9 %reshape.169 = bf16[384,30,30]{2,1,0:T(8,128)(2,1)S(1)} reshape(bf16[384,900]{1,0:T(8,128)(2,1)} %reduce-scatter.6.cloned.1.call-done) | data formatting | bytes 1382400 | tf_op jit(solution)/shard_map/while
  389.5 5.1 collective-permute-start.1
  394.6 15.6 %collective-permute-done.1 = bf16[30,30,384]{2,1,0:T(8,128)(2,1)S(1)} collective-permute-done((bf16[30,30,384]{2,1,0:T(8,128)(2,1)S(1)}, bf16[30,30,384]{2,1,0:T(8,128)(2,1)S(1)}, u32[]{:S(2)}, u32[]{:S(2)}) %collective-permute-start.1) | collective-permute-done | bytes 691232 | tf_op jit(solution)/shard_map/while/body/eval_jaxpr/ppermute | solution.py:18
  422.2 37.6 %all-gather.2.cloned.1.call-done = bf16[30,30,1536]{2,1,0:T(8,128)(2,1)} async-done(((bf16[30,30,384]{2,1,0:T(8,128)(2,1)}), bf16[30,30,1536]{2,1,0:T(8,128)(2,1)}) %all-gather.2.cloned.1.call-update) | async-done | bytes 2764816 | tf_op jit(solution)/shard_map/while/body/eval_jaxpr/all_gather | solution.py:49
  465.6 7.9 %convolution_convert_fusion.4 = bf16[900,3,384]{2,0,1:T(8,128)(2,1)} fusion(bf16[900,1536,1]{1,0,2:T(8,128)(2,1)} %reshape.166, bf16[1536,3,384]{2,0,1:T(8,128)(2,1)} %get-tuple-element.361), kind=kOutput, calls=%fused_computation.17.clone.1 | convolution fusion | flops 3186086400 | bytes 8377344 | tf_op jit(solution)/shard_map/while/body/eval_jaxpr/wtd,dcf->wtcf/dot_general | solution.py:52
  476.4 7.4 %fusion.40 = (f32[3,900]{1,0:T(4,128)S(1)}, f32[3,900,900]{1,2,0:T(8,128)}) fusion(pred[900,900]{0,1:T(8,128)(4,1)S(1)} %copy-done.1, bf16[1,900,3,3,128]{1,4,3,2,0:T(8,128)(2,1)S(1)} %bitcast.85), kind=kOutput, calls=%fused_computation.36.clone.1 | convolution fusion | flops 631800960 | bytes 12229360 | tf_op jit(solution)/shard_map/while/body/eval_jaxpr/sub | solution.py:68
  483.8 6.4 %fusion.41 = bf16[1,900,3,128]{3,1,2,0:T(8,128)(2,1)S(1)} fusion(f32[3,900,900]{1,2,0:T(8,128)} %get-tuple-element.317, f32[3,900]{1,0:T(4,128)S(1)} %get-tuple-element.318, bf16[1,900,3,3,128]{1,4,3,2,0:T(8,128)(2,1)S(1)} %bitcast.86), kind=kOutput, calls=%fused_computation.20.clone.1 | convolution fusion | flops 627285632 | bytes 11214016 | tf_op jit(solution)/shard_map/while/body/eval_jaxpr/whqk,wkhe->wqhe/dot_general | solution.py:70
  495.0 18.7 %copy.42 = bf16[30,30,1536]{1,0,2:T(8,128)(2,1)} copy(bf16[30,30,1536]{2,1,0:T(8,128)(2,1)S(1)} %convolution_convert_fusion.5) | data formatting | bytes 5529600 | tf_op jit(solution)/shard_map/while
  513.7 20.3 %reshape.168 = bf16[1536,900]{1,0:T(8,128)(2,1)} reshape(bf16[1536,30,30]{2,1,0:T(8,128)(2,1)} %bitcast.83) | data formatting | bytes 5529600 | tf_op jit(solution)/shard_map/while
  534.1 38.6 %reduce-scatter.6.cloned.1.call-done = bf16[384,900]{1,0:T(8,128)(2,1)} async-done(((bf16[1536,900]{1,0:T(8,128)(2,1)}), bf16[384,900]{1,0:T(8,128)(2,1)}) %reduce-scatter.6.cloned.1.call-update) | async-done | bytes 691216 | tf_op jit(solution)/shard_map/while
  572.6 8.9 %reshape.169 = bf16[384,30,30]{2,1,0:T(8,128)(2,1)S(1)} reshape(bf16[384,900]{1,0:T(8,128)(2,1)} %reduce-scatter.6.cloned.1.call-done) | data formatting | bytes 1382400 | tf_op jit(solution)/shard_map/while
  588.0 5.1 collective-permute-start.1
  593.0 15.6 %collective-permute-done.1 = bf16[30,30,384]{2,1,0:T(8,128)(2,1)S(1)} collective-permute-done((bf16[30,30,384]{2,1,0:T(8,128)(2,1)S(1)}, bf16[30,30,384]{2,1,0:T(8,128)(2,1)S(1)}, u32[]{:S(2)}, u32[]{:S(2)}) %collective-permute-start.1) | collective-permute-done | bytes 691232 | tf_op jit(solution)/shard_map/while/body/eval_jaxpr/ppermute | solution.py:18
  (86 shorter events, 98.8 us)
Async XLA Ops:
  6.5 3.6 copy-start.2
  10.2 52.8 %all-gather.2.cloned.1.call-start = ((), (), s32[]{:S(2)}) async-start(), calls=%async_computation.1 | async-start | bytes 3686400 | tf_op jit(solution)/shard_map/while/body/eval_jaxpr/all_gather | solution.py:49
  12.8 9.0 %collective-permute-start = (bf16[30,15,384]{2,1,0:T(8,128)(2,1)S(1)}, bf16[30,15,384]{2,1,0:T(8,128)(2,1)S(1)}, u32[]{:S(2)}, u32[]{:S(2)}) collective-permute-start(bf16[30,15,384]{2,1,0:T(8,128)(2,1)S(1)} %get-tuple-element.315), channel_id=1, source_target_pairs={{0,60},{4,0},{8,4},{12,8},{16,12},{20,16},{24,20},{28,24},{32,28},... | collective-permute-start | bytes 1036808 | tf_op jit(solution)/shard_map/while/body/eval_jaxpr/ppermute | solution.py:12
  23.1 152.6 %reduce-scatter.6.cloned.1.call-start = ((), (), s32[]{:S(2)}) async-start(), calls=%async_computation.2 | async-start | bytes 3932160 | tf_op jit(solution)/shard_map/while
  63.0 2.7 copy-start
  76.6 2.9 copy-start.1
  191.1 20.7 %collective-permute-start.1 = (bf16[30,30,384]{2,1,0:T(8,128)(2,1)S(1)}, bf16[30,30,384]{2,1,0:T(8,128)(2,1)S(1)}, u32[]{:S(2)}, u32[]{:S(2)}) collective-permute-start(bf16[30,30,384]{2,1,0:T(8,128)(2,1)S(1)} %get-tuple-element.319), channel_id=1, source_target_pairs={{0,64},{1,65},{2,66},{3,67},{4,68},{5,69},{6,70},{7,71},{8,72},{9,... | collective-permute-start | bytes 2073608 | tf_op jit(solution)/shard_map/while/body/eval_jaxpr/ppermute | solution.py:18
  211.8 49.6 %all-gather.2.cloned.1.call-start = ((), (), s32[]{:S(2)}) async-start(), calls=%async_computation.1 | async-start | bytes 3686400 | tf_op jit(solution)/shard_map/while/body/eval_jaxpr/all_gather | solution.py:49
  214.4 6.5 %collective-permute-start = (bf16[30,15,384]{2,1,0:T(8,128)(2,1)S(1)}, bf16[30,15,384]{2,1,0:T(8,128)(2,1)S(1)}, u32[]{:S(2)}, u32[]{:S(2)}) collective-permute-start(bf16[30,15,384]{2,1,0:T(8,128)(2,1)S(1)} %get-tuple-element.315), channel_id=1, source_target_pairs={{0,60},{4,0},{8,4},{12,8},{16,12},{20,16},{24,20},{28,24},{32,28},... | collective-permute-start | bytes 1036808 | tf_op jit(solution)/shard_map/while/body/eval_jaxpr/ppermute | solution.py:12
  222.1 152.1 %reduce-scatter.6.cloned.1.call-start = ((), (), s32[]{:S(2)}) async-start(), calls=%async_computation.2 | async-start | bytes 3932160 | tf_op jit(solution)/shard_map/while
  261.4 2.7 copy-start
  275.1 2.9 copy-start.1
  389.5 20.7 %collective-permute-start.1 = (bf16[30,30,384]{2,1,0:T(8,128)(2,1)S(1)}, bf16[30,30,384]{2,1,0:T(8,128)(2,1)S(1)}, u32[]{:S(2)}, u32[]{:S(2)}) collective-permute-start(bf16[30,30,384]{2,1,0:T(8,128)(2,1)S(1)} %get-tuple-element.319), channel_id=1, source_target_pairs={{0,64},{1,65},{2,66},{3,67},{4,68},{5,69},{6,70},{7,71},{8,72},{9,... | collective-permute-start | bytes 2073608 | tf_op jit(solution)/shard_map/while/body/eval_jaxpr/ppermute | solution.py:18
  410.2 49.6 %all-gather.2.cloned.1.call-start = ((), (), s32[]{:S(2)}) async-start(), calls=%async_computation.1 | async-start | bytes 3686400 | tf_op jit(solution)/shard_map/while/body/eval_jaxpr/all_gather | solution.py:49
  412.8 6.5 %collective-permute-start = (bf16[30,15,384]{2,1,0:T(8,128)(2,1)S(1)}, bf16[30,15,384]{2,1,0:T(8,128)(2,1)S(1)}, u32[]{:S(2)}, u32[]{:S(2)}) collective-permute-start(bf16[30,15,384]{2,1,0:T(8,128)(2,1)S(1)} %get-tuple-element.315), channel_id=1, source_target_pairs={{0,60},{4,0},{8,4},{12,8},{16,12},{20,16},{24,20},{28,24},{32,28},... | collective-permute-start | bytes 1036808 | tf_op jit(solution)/shard_map/while/body/eval_jaxpr/ppermute | solution.py:12
  420.6 152.1 %reduce-scatter.6.cloned.1.call-start = ((), (), s32[]{:S(2)}) async-start(), calls=%async_computation.2 | async-start | bytes 3932160 | tf_op jit(solution)/shard_map/while
  459.9 2.7 copy-start
  473.5 2.9 copy-start.1
  588.0 20.7 %collective-permute-start.1 = (bf16[30,30,384]{2,1,0:T(8,128)(2,1)S(1)}, bf16[30,30,384]{2,1,0:T(8,128)(2,1)S(1)}, u32[]{:S(2)}, u32[]{:S(2)}) collective-permute-start(bf16[30,30,384]{2,1,0:T(8,128)(2,1)S(1)} %get-tuple-element.319), channel_id=1, source_target_pairs={{0,64},{1,65},{2,66},{3,67},{4,68},{5,69},{6,70},{7,71},{8,72},{9,... | collective-permute-start | bytes 2073608 | tf_op jit(solution)/shard_map/while/body/eval_jaxpr/ppermute | solution.py:18
Sparse Core Ops, SparseCore 0:
  23.2 39.6 all-gather.1
  137.3 38.4 reduce-scatter.5
  222.2 39.1 all-gather.1
  335.7 38.4 reduce-scatter.5
  420.7 39.1 all-gather.1
  534.2 38.4 reduce-scatter.5
where the time goes:
time: 621 us; the launch traced here: 620 us
  waiting for transfers between devices  291 us (47%)
  local copies, waits for them, and re-layouts  186 us (30%)
  matrix products  74.5 us (12%)
  other arithmetic  29.7 us (5%)
  starting transfers between devices  22.3 us (4%)
  between operations  13.4 us (2%)
    while x24, local copies, waits for them, and re-layouts  156 us
    while x9, waiting for transfers between devices  116 us
    all_gather x3, waiting for transfers between devices, window_layer(): gathered = lax.all_gather(current, 'head', axis=2, tiled=True)  113 us
    ppermute x3, waiting for transfers between devices, shifted(): lax.ppermute(value, axis, [(source, source + steps) for source in range(f...  46.9 us
    dot_general x3, matrix products, window_layer(): jnp.einsum('wtd,dcf->wtcf', win_normed, qkv_local, preferred_element_type...  23.8 us
    sub x3, matrix products, window_layer(): expo = jnp.exp(scores - top_score)  22.1 us
    dot_general x3, matrix products, window_layer(): jnp.einsum('whqk,wkhe->wqhe', attn_prob, values_all, preferred_element_ty...  19.1 us
    ppermute x3, starting transfers between devices, shifted(): lax.ppermute(value, axis, [(source, source + steps) for source in range(f...  15.2 us
  transfers between devices with their start and end apart: 12, of which 12 were waited for; matrix products, arithmetic and copies ran while one was open for 1% of the time, Pallas kernels for 0%

commit v1 on v0

--- a/solution.py
+++ b/solution.py
@@ -46,7 +46,19 @@
 
 
 def window_layer(current, gain_row, qkv_local, allowed, project):
-    gathered = lax.all_gather(current, "head", axis=2, tiled=True)
+
+    def trace_outputs_on_mesh(state, pos_dim=2):
+        return jnp.concatenate(
+            lax.all_to_all(
+                jnp.stack([state for _ in range(lax.axis_size("head"))]),
+                axis_name="head",
+                split_axis=0,
+                concat_axis=0,
+            ),
+            pos_dim,
+        )
+
+    gathered = trace_outputs_on_mesh(current)
     normed = rms_normed(gathered, gain_row)
     win_normed = to_windows(normed)
     projected_qkv = jnp.einsum(

time: 621 us -> 640 us (1.031)
  local copies, waits for them, and re-layouts: 186 us -> 213 us
  waiting for transfers between devices: 291 us -> 277 us
  starting transfers between devices: 22.3 us -> 33.9 us
  other arithmetic: 29.7 us -> 21.3 us
    all_gather x3 -> x0, waiting for transfers between devices: 113 us -> none  [window_layer(): gathered = lax.all_gather(current, 'head', axis=2, tiled=True)]
    all_to_all x0 -> x3, waiting for transfers between devices: none -> 100 us  [trace_outputs_on_mesh(): lax.all_to_all(jnp.stack([state for _ in range(lax.axis_size('head'))]),...]
    convert_element_type x0 -> x3, local copies, waits for them, and re-layouts: none -> 13.8 us  [rms_normed(): values_f = slab.astype(jnp.float32)]
    while x24 -> x30, local copies, waits for them, and re-layouts: 156 us -> 170 us
    all_to_all x0 -> x3, starting transfers between devices: none -> 11.7 us  [trace_outputs_on_mesh(): lax.all_to_all(jnp.stack([state for _ in range(lax.axis_size('head'))]),...]
    while x9 -> x6, waiting for transfers between devices: 116 us -> 115 us
where the time goes in v1:
time: 640 us; the launch traced here: 638 us
  waiting for transfers between devices  277 us (43%)
  local copies, waits for them, and re-layouts  213 us (33%)
  matrix products  77.7 us (12%)
  starting transfers between devices  33.9 us (5%)
  other arithmetic  21.3 us (3%)
  between operations  13.1 us (2%)
    while x30, local copies, waits for them, and re-layouts  170 us
    while x6, waiting for transfers between devices  115 us
    all_to_all x3, waiting for transfers between devices, trace_outputs_on_mesh(): lax.all_to_all(jnp.stack([state for _ in range(lax.axis_size('head'))]),...  100 us
    ppermute x3, waiting for transfers between devices, shifted(): lax.ppermute(value, axis, [(source, source + steps) for source in range(f...  46.9 us
    dot_general x3, matrix products, window_layer(): jnp.einsum('wtd,dcf->wtcf', win_normed, qkv_local, preferred_element_type...  26.8 us
    sub x3, matrix products, window_layer(): expo = jnp.exp(scores - top_score)  22.3 us
    dot_general x3, matrix products, window_layer(): jnp.einsum('whqk,wkhe->wqhe', attn_prob, values_all, preferred_element_ty...  19.1 us
    ppermute x3, starting transfers between devices, shifted(): lax.ppermute(value, axis, [(source, source + steps) for source in range(f...  15.3 us
  transfers between devices with their start and end apart: 12, of which 12 were waited for; matrix products, arithmetic and copies ran while one was open for 1% of the time, Pallas kernels for 0%

profile of v1, /device:TPU:0, one launch (start us, length us, event | category | flops | bytes accessed | tf_op | source)
XLA Modules:
  0.0 638.2 jit_solution(2694059572702554380)
XLA Ops:
  10.2 617.5 %while.16 = (s32[]{:T(128)}, bf16[30,30,384]{2,1,0:T(8,128)(2,1)S(1)}, bf16[3,30,30,384]{3,2,1,0:T(8,128)(2,1)}, pred[]{:T(512)}, pred[]{:T(512)}, /*index=5*/s3...) while((s32[]{:T(128)}, ...), condition=%wide.region_5.6_spmd.clone.clone, body=%wide.region_0.5_spmd.clone.clone.sunk | while | flops 5522992128 | bytes 146670096 | solution.py:122
  16.8 5.0 collective-permute-done
  30.8 32.4 %all-to-all-done = bf16[4,30,30,384]{3,2,1,0:T(8,128)(2,1)S(1)} async-done(((bf16[4,30,30,384]{3,2,1,0:T(8,128)(2,1)}), bf16[4,30,30,384]{3,2,1,0:T(8,128)(2,1)S(1)}, u32[]{:S(2)}, u32[]{:S(2)}) %all-to-all-start) | async-done | bytes 2764832 | tf_op jit(solution)/shard_map/while/body/eval_jaxpr/all_to_all | solution.py:52
  73.3 8.9 %fusion.44 = bf16[900,3,384]{2,0,1:T(8,128)(2,1)} fusion(bf16[1536,3,384]{2,0,1:T(8,128)(2,1)} %get-tuple-element.374, f32[900,1536]{1,0:T(8,128)} %bitcast.105, f32[1536]{0:T(1024)S(1)} %reduce.12, f32[900]{0:T(1024)S(1)} %rsqrt.21), kind=kOutput, calls=%fused_computation.20.clone.1 | convolution fusion | flops 3190233600 | bytes 11151888 | tf_op jit(solution)/shard_map/while/body/eval_jaxpr/wtd,dcf->wtcf/dot_general | solution.py:64
  85.1 7.4 %fusion.45 = (f32[3,900]{1,0:T(4,128)S(1)}, f32[3,900,900]{1,2,0:T(8,128)}) fusion(pred[900,900]{0,1:T(8,128)(4,1)S(1)} %copy-done.1, bf16[1,900,3,3,128]{1,4,3,2,0:T(8,128)(2,1)S(1)} %bitcast.106), kind=kOutput, calls=%fused_computation.39.clone.1 | convolution fusion | flops 631800960 | bytes 12229360 | tf_op jit(solution)/shard_map/while/body/eval_jaxpr/sub | solution.py:80
  92.5 6.4 fusion.46
  103.8 18.7 %copy.56 = bf16[30,30,1536]{1,0,2:T(8,128)(2,1)} copy(bf16[30,30,1536]{2,1,0:T(8,128)(2,1)S(1)} %convolution_convert_fusion.2) | data formatting | bytes 5529600 | tf_op jit(solution)/shard_map/while
  122.5 20.3 %reshape.183 = bf16[1536,900]{1,0:T(8,128)(2,1)} reshape(bf16[1536,30,30]{2,1,0:T(8,128)(2,1)} %bitcast.101) | data formatting | bytes 5529600 | tf_op jit(solution)/shard_map/while
  142.8 38.5 %reduce-scatter.6.cloned.1.call-done = bf16[384,900]{1,0:T(8,128)(2,1)} async-done(((bf16[1536,900]{1,0:T(8,128)(2,1)}), bf16[384,900]{1,0:T(8,128)(2,1)}) %reduce-scatter.6.cloned.1.call-update) | async-done | bytes 691216 | tf_op jit(solution)/shard_map/while
  181.3 8.9 %reshape.184 = bf16[384,30,30]{2,1,0:T(8,128)(2,1)S(1)} reshape(bf16[384,900]{1,0:T(8,128)(2,1)} %reduce-scatter.6.cloned.1.call-done) | data formatting | bytes 1382400 | tf_op jit(solution)/shard_map/while
  196.7 5.1 collective-permute-start.1
  201.8 15.6 %collective-permute-done.1 = bf16[30,30,384]{2,1,0:T(8,128)(2,1)S(1)} collective-permute-done((bf16[30,30,384]{2,1,0:T(8,128)(2,1)S(1)}, bf16[30,30,384]{2,1,0:T(8,128)(2,1)S(1)}, u32[]{:S(2)}, u32[]{:S(2)}) %collective-permute-start.1) | collective-permute-done | bytes 691232 | tf_op jit(solution)/shard_map/while/body/eval_jaxpr/ppermute | solution.py:18
  234.9 33.8 %all-to-all-done = bf16[4,30,30,384]{3,2,1,0:T(8,128)(2,1)S(1)} async-done(((bf16[4,30,30,384]{3,2,1,0:T(8,128)(2,1)}), bf16[4,30,30,384]{3,2,1,0:T(8,128)(2,1)S(1)}, u32[]{:S(2)}, u32[]{:S(2)}) %all-to-all-start) | async-done | bytes 2764832 | tf_op jit(solution)/shard_map/while/body/eval_jaxpr/all_to_all | solution.py:52
  278.8 8.9 %fusion.44 = bf16[900,3,384]{2,0,1:T(8,128)(2,1)} fusion(bf16[1536,3,384]{2,0,1:T(8,128)(2,1)} %get-tuple-element.374, f32[900,1536]{1,0:T(8,128)} %bitcast.105, f32[1536]{0:T(1024)S(1)} %reduce.12, f32[900]{0:T(1024)S(1)} %rsqrt.21), kind=kOutput, calls=%fused_computation.20.clone.1 | convolution fusion | flops 3190233600 | bytes 11151888 | tf_op jit(solution)/shard_map/while/body/eval_jaxpr/wtd,dcf->wtcf/dot_general | solution.py:64
  290.6 7.4 %fusion.45 = (f32[3,900]{1,0:T(4,128)S(1)}, f32[3,900,900]{1,2,0:T(8,128)}) fusion(pred[900,900]{0,1:T(8,128)(4,1)S(1)} %copy-done.1, bf16[1,900,3,3,128]{1,4,3,2,0:T(8,128)(2,1)S(1)} %bitcast.106), kind=kOutput, calls=%fused_computation.39.clone.1 | convolution fusion | flops 631800960 | bytes 12229360 | tf_op jit(solution)/shard_map/while/body/eval_jaxpr/sub | solution.py:80
  298.0 6.4 fusion.46
  309.3 18.7 %copy.56 = bf16[30,30,1536]{1,0,2:T(8,128)(2,1)} copy(bf16[30,30,1536]{2,1,0:T(8,128)(2,1)S(1)} %convolution_convert_fusion.2) | data formatting | bytes 5529600 | tf_op jit(solution)/shard_map/while
  328.0 20.3 %reshape.183 = bf16[1536,900]{1,0:T(8,128)(2,1)} reshape(bf16[1536,30,30]{2,1,0:T(8,128)(2,1)} %bitcast.101) | data formatting | bytes 5529600 | tf_op jit(solution)/shard_map/while
  348.3 38.2 %reduce-scatter.6.cloned.1.call-done = bf16[384,900]{1,0:T(8,128)(2,1)} async-done(((bf16[1536,900]{1,0:T(8,128)(2,1)}), bf16[384,900]{1,0:T(8,128)(2,1)}) %reduce-scatter.6.cloned.1.call-update) | async-done | bytes 691216 | tf_op jit(solution)/shard_map/while
  386.5 8.9 %reshape.184 = bf16[384,30,30]{2,1,0:T(8,128)(2,1)S(1)} reshape(bf16[384,900]{1,0:T(8,128)(2,1)} %reduce-scatter.6.cloned.1.call-done) | data formatting | bytes 1382400 | tf_op jit(solution)/shard_map/while
  401.8 5.1 collective-permute-start.1
  406.9 15.6 %collective-permute-done.1 = bf16[30,30,384]{2,1,0:T(8,128)(2,1)S(1)} collective-permute-done((bf16[30,30,384]{2,1,0:T(8,128)(2,1)S(1)}, bf16[30,30,384]{2,1,0:T(8,128)(2,1)S(1)}, u32[]{:S(2)}, u32[]{:S(2)}) %collective-permute-start.1) | collective-permute-done | bytes 691232 | tf_op jit(solution)/shard_map/while/body/eval_jaxpr/ppermute | solution.py:18
  440.1 33.8 %all-to-all-done = bf16[4,30,30,384]{3,2,1,0:T(8,128)(2,1)S(1)} async-done(((bf16[4,30,30,384]{3,2,1,0:T(8,128)(2,1)}), bf16[4,30,30,384]{3,2,1,0:T(8,128)(2,1)S(1)}, u32[]{:S(2)}, u32[]{:S(2)}) %all-to-all-start) | async-done | bytes 2764832 | tf_op jit(solution)/shard_map/while/body/eval_jaxpr/all_to_all | solution.py:52
  483.9 8.9 %fusion.44 = bf16[900,3,384]{2,0,1:T(8,128)(2,1)} fusion(bf16[1536,3,384]{2,0,1:T(8,128)(2,1)} %get-tuple-element.374, f32[900,1536]{1,0:T(8,128)} %bitcast.105, f32[1536]{0:T(1024)S(1)} %reduce.12, f32[900]{0:T(1024)S(1)} %rsqrt.21), kind=kOutput, calls=%fused_computation.20.clone.1 | convolution fusion | flops 3190233600 | bytes 11151888 | tf_op jit(solution)/shard_map/while/body/eval_jaxpr/wtd,dcf->wtcf/dot_general | solution.py:64
  495.7 7.4 %fusion.45 = (f32[3,900]{1,0:T(4,128)S(1)}, f32[3,900,900]{1,2,0:T(8,128)}) fusion(pred[900,900]{0,1:T(8,128)(4,1)S(1)} %copy-done.1, bf16[1,900,3,3,128]{1,4,3,2,0:T(8,128)(2,1)S(1)} %bitcast.106), kind=kOutput, calls=%fused_computation.39.clone.1 | convolution fusion | flops 631800960 | bytes 12229360 | tf_op jit(solution)/shard_map/while/body/eval_jaxpr/sub | solution.py:80
  503.2 6.4 fusion.46
  514.5 18.7 %copy.56 = bf16[30,30,1536]{1,0,2:T(8,128)(2,1)} copy(bf16[30,30,1536]{2,1,0:T(8,128)(2,1)S(1)} %convolution_convert_fusion.2) | data formatting | bytes 5529600 | tf_op jit(solution)/shard_map/while
  533.1 20.3 %reshape.183 = bf16[1536,900]{1,0:T(8,128)(2,1)} reshape(bf16[1536,30,30]{2,1,0:T(8,128)(2,1)} %bitcast.101) | data formatting | bytes 5529600 | tf_op jit(solution)/shard_map/while
  553.5 38.2 %reduce-scatter.6.cloned.1.call-done = bf16[384,900]{1,0:T(8,128)(2,1)} async-done(((bf16[1536,900]{1,0:T(8,128)(2,1)}), bf16[384,900]{1,0:T(8,128)(2,1)}) %reduce-scatter.6.cloned.1.call-update) | async-done | bytes 691216 | tf_op jit(solution)/shard_map/while
  591.6 8.9 %reshape.184 = bf16[384,30,30]{2,1,0:T(8,128)(2,1)S(1)} reshape(bf16[384,900]{1,0:T(8,128)(2,1)} %reduce-scatter.6.cloned.1.call-done) | data formatting | bytes 1382400 | tf_op jit(solution)/shard_map/while
  607.0 5.1 collective-permute-start.1
  612.1 15.6 %collective-permute-done.1 = bf16[30,30,384]{2,1,0:T(8,128)(2,1)S(1)} collective-permute-done((bf16[30,30,384]{2,1,0:T(8,128)(2,1)S(1)}, bf16[30,30,384]{2,1,0:T(8,128)(2,1)S(1)}, u32[]{:S(2)}, u32[]{:S(2)}) %collective-permute-start.1) | collective-permute-done | bytes 691232 | tf_op jit(solution)/shard_map/while/body/eval_jaxpr/ppermute | solution.py:18
  (95 shorter events, 128.9 us)
Async XLA Ops:
  6.5 3.6 copy-start.2
  12.8 9.0 %collective-permute-start = (bf16[30,15,384]{2,1,0:T(8,128)(2,1)S(1)}, bf16[30,15,384]{2,1,0:T(8,128)(2,1)S(1)}, u32[]{:S(2)}, u32[]{:S(2)}) collective-permute-start(bf16[30,15,384]{2,1,0:T(8,128)(2,1)S(1)} %get-tuple-element.326), channel_id=1, source_target_pairs={{0,60},{4,0},{8,4},{12,8},{16,12},{20,16},{24,20},{28,24},{32,28},... | collective-permute-start | bytes 1036808 | tf_op jit(solution)/shard_map/while/body/eval_jaxpr/ppermute | solution.py:12
  22.1 0.9 copy-start
  24.9 38.3 %all-to-all-start = ((bf16[4,30,30,384]{3,2,1,0:T(8,128)(2,1)}), bf16[4,30,30,384]{3,2,1,0:T(8,128)(2,1)S(1)}, u32[]{:S(2)}, u32[]{:S(2)}) async-start(bf16[4,30,30,384]{3,2,1,0:T(8,128)(2,1)} %stack.10), calls=%async_computation | async-start | bytes 5898240 | tf_op jit(solution)/shard_map/while/body/eval_jaxpr/all_to_all | solution.py:52
  29.2 152.1 %reduce-scatter.6.cloned.1.call-start = ((), (), s32[]{:S(2)}) async-start(), calls=%async_computation.2 | async-start | bytes 3932160 | tf_op jit(solution)/shard_map/while
  82.2 2.9 copy-start.1
  196.7 20.7 %collective-permute-start.1 = (bf16[30,30,384]{2,1,0:T(8,128)(2,1)S(1)}, bf16[30,30,384]{2,1,0:T(8,128)(2,1)S(1)}, u32[]{:S(2)}, u32[]{:S(2)}) collective-permute-start(bf16[30,30,384]{2,1,0:T(8,128)(2,1)S(1)} %get-tuple-element.330), channel_id=1, source_target_pairs={{0,64},{1,65},{2,66},{3,67},{4,68},{5,69},{6,70},{7,71},{8,72},{9,... | collective-permute-start | bytes 2073608 | tf_op jit(solution)/shard_map/while/body/eval_jaxpr/ppermute | solution.py:18
  220.0 6.5 %collective-permute-start = (bf16[30,15,384]{2,1,0:T(8,128)(2,1)S(1)}, bf16[30,15,384]{2,1,0:T(8,128)(2,1)S(1)}, u32[]{:S(2)}, u32[]{:S(2)}) collective-permute-start(bf16[30,15,384]{2,1,0:T(8,128)(2,1)S(1)} %get-tuple-element.326), channel_id=1, source_target_pairs={{0,60},{4,0},{8,4},{12,8},{16,12},{20,16},{24,20},{28,24},{32,28},... | collective-permute-start | bytes 1036808 | tf_op jit(solution)/shard_map/while/body/eval_jaxpr/ppermute | solution.py:12
  226.8 0.9 copy-start
  229.6 39.1 %all-to-all-start = ((bf16[4,30,30,384]{3,2,1,0:T(8,128)(2,1)}), bf16[4,30,30,384]{3,2,1,0:T(8,128)(2,1)S(1)}, u32[]{:S(2)}, u32[]{:S(2)}) async-start(bf16[4,30,30,384]{3,2,1,0:T(8,128)(2,1)} %stack.10), calls=%async_computation | async-start | bytes 5898240 | tf_op jit(solution)/shard_map/while/body/eval_jaxpr/all_to_all | solution.py:52
  233.3 153.2 %reduce-scatter.6.cloned.1.call-start = ((), (), s32[]{:S(2)}) async-start(), calls=%async_computation.2 | async-start | bytes 3932160 | tf_op jit(solution)/shard_map/while
  287.7 2.9 copy-start.1
  401.8 20.7 %collective-permute-start.1 = (bf16[30,30,384]{2,1,0:T(8,128)(2,1)S(1)}, bf16[30,30,384]{2,1,0:T(8,128)(2,1)S(1)}, u32[]{:S(2)}, u32[]{:S(2)}) collective-permute-start(bf16[30,30,384]{2,1,0:T(8,128)(2,1)S(1)} %get-tuple-element.330), channel_id=1, source_target_pairs={{0,64},{1,65},{2,66},{3,67},{4,68},{5,69},{6,70},{7,71},{8,72},{9,... | collective-permute-start | bytes 2073608 | tf_op jit(solution)/shard_map/while/body/eval_jaxpr/ppermute | solution.py:18
  425.1 6.5 %collective-permute-start = (bf16[30,15,384]{2,1,0:T(8,128)(2,1)S(1)}, bf16[30,15,384]{2,1,0:T(8,128)(2,1)S(1)}, u32[]{:S(2)}, u32[]{:S(2)}) collective-permute-start(bf16[30,15,384]{2,1,0:T(8,128)(2,1)S(1)} %get-tuple-element.326), channel_id=1, source_target_pairs={{0,60},{4,0},{8,4},{12,8},{16,12},{20,16},{24,20},{28,24},{32,28},... | collective-permute-start | bytes 1036808 | tf_op jit(solution)/shard_map/while/body/eval_jaxpr/ppermute | solution.py:12
  431.9 0.9 copy-start
  434.7 39.1 %all-to-all-start = ((bf16[4,30,30,384]{3,2,1,0:T(8,128)(2,1)}), bf16[4,30,30,384]{3,2,1,0:T(8,128)(2,1)S(1)}, u32[]{:S(2)}, u32[]{:S(2)}) async-start(bf16[4,30,30,384]{3,2,1,0:T(8,128)(2,1)} %stack.10), calls=%async_computation | async-start | bytes 5898240 | tf_op jit(solution)/shard_map/while/body/eval_jaxpr/all_to_all | solution.py:52
  438.4 153.2 %reduce-scatter.6.cloned.1.call-start = ((), (), s32[]{:S(2)}) async-start(), calls=%async_computation.2 | async-start | bytes 3932160 | tf_op jit(solution)/shard_map/while
  492.9 2.9 copy-start.1
  607.0 20.7 %collective-permute-start.1 = (bf16[30,30,384]{2,1,0:T(8,128)(2,1)S(1)}, bf16[30,30,384]{2,1,0:T(8,128)(2,1)S(1)}, u32[]{:S(2)}, u32[]{:S(2)}) collective-permute-start(bf16[30,30,384]{2,1,0:T(8,128)(2,1)S(1)} %get-tuple-element.330), channel_id=1, source_target_pairs={{0,64},{1,65},{2,66},{3,67},{4,68},{5,69},{6,70},{7,71},{8,72},{9,... | collective-permute-start | bytes 2073608 | tf_op jit(solution)/shard_map/while/body/eval_jaxpr/ppermute | solution.py:18
Sparse Core Ops, SparseCore 0:
  142.9 38.2 reduce-scatter.5
  348.4 38.0 reduce-scatter.5
  553.6 38.0 reduce-scatter.5
